TPU v7x, 128 devices: a whole 4x4x4 slice. The times are simulated.
128 devices in a mesh: child: 2 (over z_lo), row: 16 (over x, y), col: 4 (over z_hi, core).
Axes of the slice: x: 4, y: 4, z: 4 (z_hi: 2, z_lo: 2; z = z_hi * 2 + z_lo), core: 2. Of those that a mesh axis runs over, the one named last changes fastest.
Arguments:
- child_fronts: float32 [2, 4096, 4096], P('child', 'row', 'col'), as said below
- root_front: float32 [8192, 8192], P('col', ('child', 'row')), as said below
- block_maps: int32 [2, 24], replicated, may hold values from 0 to 63, as said below
Outputs:
- child_factor: float32 [2, 4096, 1024], P('child', 'row')
- root_factor: float32 [8192, 512], P('col')
- root_trailing: float32 [8192, 8192], P('col', ('child', 'row'))
Inputs may be any that keep to these rules, and one draw needn't show every extreme that they name: `block_maps`: row c lists 24 different root blocks in increasing order; block 0 appears in the first row and the last root block in the last row. `child_fronts`: each front is symmetric and positive definite. `root_front`: symmetric and positive definite.
All inputs are finite; a program needn't handle non-finite values.
Results may differ from a plain program's by a relative error of at most 0.0003.
Values may be sent and summed in bfloat16 or wider, within the bound.
No kernel may reach another device: no remote copies, remote signals or barrier semaphores. Data moves between devices by JAX's collectives and lax.ppermute only.
A program may use at most 128 MiB of HBM per device.

v0:
```python
import jax
import jax.numpy as jnp
from jax import lax
from jax.sharding import PartitionSpec as P

R = 8192
PANEL = 512
CPAN = 2
BLK = 128
PIV = 1024
NCB = 24


def from_root(block, axis, holder):
    block = jnp.where(lax.axis_index(axis) == holder, block, jnp.zeros_like(block))
    return lax.psum(block, axis)


def lookup(table, first_idx, second_idx):
    hits = (first_idx[..., None, None] == jnp.arange(table.shape[0], dtype=jnp.int32)[:, None]) & (
        second_idx[..., None, None] == jnp.arange(table.shape[1], dtype=jnp.int32)[None, :]
    )
    return jnp.sum(jnp.where(hits, table, 0), axis=(-2, -1))


def panel_step(local_tile, first_col, is_root):
    row_block, col_block = local_tile.shape
    if is_root:
        row_pos = lax.axis_index("col")
        col_pos = lax.axis_index(("child", "row"))
    else:
        row_pos = lax.axis_index("row")
        col_pos = lax.axis_index("col")
    panel_width = min(PANEL, col_block)
    offset = first_col % col_block if col_block >= PANEL else 0
    portion = lax.slice_in_dim(local_tile, offset, offset + panel_width, axis=1)
    arrived = []
    for member in range(max(PANEL // col_block, 1)):
        holder = first_col // col_block + member
        if is_root:
            arrived.append(from_root(portion, ("child", "row"), holder))
        else:
            arrived.append(from_root(portion, "col", holder))
    panel_rows = jnp.concatenate(arrived, axis=1)
    diag_width = min(PANEL, row_block)
    diag_offset = first_col % row_block if row_block >= PANEL else 0
    diag_portion = lax.slice_in_dim(panel_rows, diag_offset, diag_offset + diag_width, axis=0)
    diag_parts = []
    for member in range(max(PANEL // row_block, 1)):
        holder = first_col // row_block + member
        if is_root:
            diag_parts.append(from_root(diag_portion, "col", holder))
        else:
            diag_parts.append(from_root(diag_portion, "row", holder))
    diagonal = jnp.concatenate(diag_parts, axis=0)
    diag_factor = jnp.linalg.cholesky(diagonal)
    solved = lax.linalg.triangular_solve(
        diag_factor, panel_rows, left_side=False, lower=True, transpose_a=True
    )
    row_ids = row_pos * row_block + jnp.arange(row_block, dtype=jnp.int32)
    factor_rows = jnp.where(row_ids[:, None] >= first_col, solved, 0.0)
    update_rows = jnp.where(row_ids[:, None] >= first_col + PANEL, solved, 0.0).astype(jnp.bfloat16)
    if is_root:
        all_rows = lax.all_gather(update_rows, "col", axis=0, tiled=True)
    else:
        all_rows = lax.all_gather(update_rows, "row", axis=0, tiled=True)
    column_rows = lax.dynamic_slice_in_dim(all_rows, col_pos * col_block, col_block, 0)
    update = lax.dot_general(
        update_rows, column_rows, (((1,), (1,)), ((), ())), preferred_element_type=jnp.float32
    )
    return (local_tile - update, factor_rows)


def local(child_fronts, root_front, block_maps):
    local_tile = child_fronts[0]
    factors = []
    for panel_index in range(CPAN):
        local_tile, factor_rows = panel_step(local_tile, panel_index * PANEL, False)
        factors.append(factor_rows)
    child_factor = jnp.concatenate(factors, axis=1)[None]
    row_block, col_block = local_tile.shape
    child_pos = lax.axis_index("child")
    col_pos = lax.axis_index("col")
    row_count = lax.axis_size("row")
    group_count = lax.axis_size(("child", "row"))
    col_count = lax.axis_size("col")
    row_blocks = row_block // BLK
    root_blocks = R // BLK
    target_blocks = R // col_count // BLK
    width_out = R // group_count
    sources = jnp.arange(group_count, dtype=jnp.int32)
    front_blocks = (sources % row_count)[:, None] * row_blocks + jnp.arange(
        row_blocks, dtype=jnp.int32
    )[None, :]
    contrib_rows = front_blocks - PIV // BLK
    source_child = jnp.broadcast_to((sources // row_count)[:, None], contrib_rows.shape)
    row_targets = lookup(block_maps, source_child, contrib_rows)
    row_valid = contrib_rows >= 0
    block_ids = jnp.arange(root_blocks, dtype=jnp.int32)
    full_rows = lax.all_gather(local_tile, "col", axis=1, tiled=True)
    contrib = full_rows[:, PIV:].reshape(row_block, NCB, BLK)
    col_targets = lookup(
        block_maps, jnp.full((NCB,), child_pos, dtype=jnp.int32), jnp.arange(NCB, dtype=jnp.int32)
    )
    col_table = (col_targets[:, None] == block_ids[None, :]).astype(jnp.float32)
    placed = jnp.einsum("ray,am->rmy", contrib, col_table, precision=lax.Precision.HIGHEST).reshape(
        row_block, group_count, width_out
    )
    keep_rows = row_valid & (row_targets // target_blocks == col_pos)
    row_table = (
        keep_rows[:, :, None]
        & (
            (row_targets % target_blocks)[:, :, None]
            == jnp.arange(target_blocks, dtype=jnp.int32)[None, None, :]
        )
    ).astype(jnp.float32)
    received = lax.all_to_all(placed, ("child", "row"), split_axis=1, concat_axis=0, tiled=True)
    count_cols = received.shape[2]
    stacked = received.reshape(group_count, row_blocks, BLK, count_cols)
    summed = jnp.einsum("stq,stxn->qxn", row_table, stacked, precision=lax.Precision.HIGHEST)
    added = summed.reshape(target_blocks * BLK, count_cols)
    assembled = root_front + added
    panel_index = 0
    assembled, factor_rows = panel_step(assembled, panel_index * PANEL, True)
    return (child_factor, factor_rows, assembled)


def solution(mesh):
    return jax.shard_map(
        local,
        mesh=mesh,
        in_specs=(P("child", "row", "col"), P("col", ("child", "row")), P()),
        out_specs=(P("child", "row", None), P("col", None), P("col", ("child", "row"))),
        check_vma=False,
    )
```

profile of v0, /device:TPU:1, one launch (start us, length us, event | category | flops | bytes accessed | tf_op | source)
XLA Modules:
  0.0 1564.4 jit_solution(4274154260043947339)
XLA Ops:
  9.7 47.3 %all-reduce.11.cloned.1.call-done = f32[256,512]{0,1:T(8,128)} async-done(((f32[256,512]{0,1:T(8,128)}), f32[256,512]{0,1:T(8,128)}) %all-reduce.11.cloned.1.call-update) | async-done | bytes 524304 | tf_op jit(solution)/shard_map/psum | solution.py:16
  59.1 85.8 %all-reduce.21.cloned.1.call-done = (f32[256,512]{0,1:T(8,128)}, f32[256,512]{0,1:T(8,128)}) async-done(((f32[256,512]{0,1:T(8,128)}, f32[256,512]{0,1:T(8,128)}), (f32[256,512]{0,1:T(8,128)}, f32[256,512]{0,1:T(8,128)})) %all-reduce.21.cloned.1.call-update) | async-done | bytes 1048592 | tf_op jit(solution)/shard_map/psum | solution.py:16
  148.8 11.7 cholesky.374
  173.0 11.7 cholesky.393
  196.3 11.7 cholesky.414
  220.1 11.7 cholesky.431
  232.4 12.5 compare_reduce_fusion.10
  255.7 39.3 %custom-call.37 = f32[4,128,128]{1,2,0:T(8,128)S(1)} custom-call(f32[4,128,128]{2,1,0:T(8,128)S(1)} %get-tuple-element.27), custom_call_target="InvertDiagBlocksLowerTriangular" | custom-call | tf_op jit(solution)/shard_map/triangular_solve/custom-call.3 | solution.py:57
  301.9 57.4 %all-gather.5.cloned.1.call-done = bf16[4096,512]{0,1:T(8,128)(2,1)} async-done(((bf16[256,512]{0,1:T(8,128)(2,1)}), bf16[4096,512]{0,1:T(8,128)(2,1)}) %all-gather.5.cloned.1.call-update) | async-done | bytes 4194320 | tf_op jit(solution)/shard_map/all_gather | solution.py:66
  362.0 43.1 %all-reduce.13.cloned.1.call-done = f32[256,512]{0,1:T(8,128)} async-done(((f32[256,512]{0,1:T(8,128)}), f32[256,512]{0,1:T(8,128)}) %all-reduce.13.cloned.1.call-update) | async-done | bytes 524304 | tf_op jit(solution)/shard_map/psum | solution.py:16
  407.9 85.2 %all-reduce.19.cloned.1.call-done = (f32[256,512]{0,1:T(8,128)}, f32[256,512]{0,1:T(8,128)}) async-done(((f32[256,512]{0,1:T(8,128)}, f32[256,512]{0,1:T(8,128)}), (f32[256,512]{0,1:T(8,128)}, f32[256,512]{0,1:T(8,128)})) %all-reduce.19.cloned.1.call-update) | async-done | bytes 1048592 | tf_op jit(solution)/shard_map/psum | solution.py:16
  496.8 11.7 cholesky.446
  521.0 11.7 cholesky.465
  592.8 39.3 %custom-call.41 = f32[4,128,128]{1,2,0:T(8,128)S(1)} custom-call(f32[4,128,128]{2,1,0:T(8,128)S(1)} %get-tuple-element.28), custom_call_target="InvertDiagBlocksLowerTriangular" | custom-call | tf_op jit(solution)/shard_map/triangular_solve/custom-call.3 | solution.py:57
  639.6 57.4 %all-gather.7.cloned.1.call-done = bf16[4096,512]{0,1:T(8,128)(2,1)} async-done(((bf16[256,512]{0,1:T(8,128)(2,1)}), bf16[4096,512]{0,1:T(8,128)(2,1)}) %all-gather.7.cloned.1.call-update) | async-done | bytes 4194320 | tf_op jit(solution)/shard_map/all_gather | solution.py:66
  700.1 39.3 %all-gather.9.cloned.1.call-done = f32[256,4096]{0,1:T(8,128)} async-done(((f32[256,1024]{0,1:T(8,128)}), f32[256,4096]{0,1:T(8,128)}) %all-gather.9.cloned.1.call-update) | async-done | bytes 4194320 | tf_op jit(solution)/shard_map/all_gather | solution.py:100
  783.2 115.7 %all-to-all-done = f32[256,32,256]{2,0,1:T(8,128)} async-done(((f32[256,32,256]{2,0,1:T(8,128)}), f32[256,32,256]{2,0,1:T(8,128)}, u32[]{:S(2)}, u32[]{:S(2)}) %all-to-all-start) | async-done | bytes 8388640 | tf_op jit(solution)/shard_map/all_to_all | solution.py:117
  917.8 312.3 %all-reduce.17.cloned.1.call-done = (f32[2048,256]{0,1:T(8,128)}, f32[2048,256]{0,1:T(8,128)}) async-done(((f32[2048,256]{0,1:T(8,128)}, f32[2048,256]{0,1:T(8,128)}), (f32[2048,256]{0,1:T(8,128)}, f32[2048,256]{0,1:T(8,128)})) %all-reduce.17.cloned.1.call-update) | async-done | bytes 4194320 | tf_op jit(solution)/shard_map/psum | solution.py:16
  1232.5 68.1 %all-reduce.15.cloned.1.call-done = f32[512,512]{0,1:T(8,128)} async-done(((f32[512,512]{0,1:T(8,128)}), f32[512,512]{0,1:T(8,128)}) %all-reduce.15.cloned.1.call-update) | async-done | bytes 1048592 | tf_op jit(solution)/shard_map/psum | solution.py:16
  1360.7 13.2 cholesky.558
  1392.7 13.2 cholesky.575
  1418.0 12.0 while.5
  1430.1 40.1 %custom-call.26 = f32[4,128,128]{1,2,0:T(8,128)} custom-call(f32[4,128,128]{2,1,0:T(8,128)S(1)} %get-tuple-element.20), custom_call_target="InvertDiagBlocksLowerTriangular" | custom-call | tf_op jit(solution)/shard_map/triangular_solve | solution.py:57
  1502.9 46.4 %all-gather.11.cloned.1.call-done = bf16[8192,512]{0,1:T(8,128)(2,1)} async-done(((bf16[2048,512]{0,1:T(8,128)(2,1)}), bf16[8192,512]{0,1:T(8,128)(2,1)}) %all-gather.11.cloned.1.call-update) | async-done | bytes 8388624 | tf_op jit(solution)/shard_map/all_gather | solution.py:64
  (261 shorter events, 371.0 us)
Async XLA Ops:
  7.2 49.8 %all-reduce.11.cloned.1.call-start = ((), (), s32[]{:S(2)}) async-start(), calls=%async_computation.1 | async-start | bytes 1048576 | tf_op jit(solution)/shard_map/psum | solution.py:16
  9.6 135.3 %all-reduce.21.cloned.1.call-start = ((), (), s32[]{:S(2)}) async-start(), calls=%async_computation.10 | async-start | bytes 2097152 | tf_op jit(solution)/shard_map/psum | solution.py:16
  59.1 300.2 %all-gather.5.cloned.1.call-start = ((), (), s32[]{:S(2)}) async-start(), calls=%async_computation.2 | async-start | bytes 4456448 | tf_op jit(solution)/shard_map/all_gather | solution.py:66
  299.3 62.6 %copy-start.9 = (f32[256,128]{0,1:T(8,128)}, f32[256,128]{0,1:T(8,128)S(1)}, u32[]{:S(2)}) copy-start(f32[256,128]{0,1:T(8,128)S(1)} %fusion.81) | copy-start | bytes 393220
  301.8 103.3 %all-reduce.13.cloned.1.call-start = ((), (), s32[]{:S(2)}) async-start(), calls=%async_computation.3 | async-start | bytes 1048576 | tf_op jit(solution)/shard_map/psum | solution.py:16
  362.0 131.0 %all-reduce.19.cloned.1.call-start = ((), (), s32[]{:S(2)}) async-start(), calls=%async_computation.9 | async-start | bytes 2097152 | tf_op jit(solution)/shard_map/psum | solution.py:16
  407.3 289.8 %all-gather.7.cloned.1.call-start = ((), (), s32[]{:S(2)}) async-start(), calls=%async_computation.4 | async-start | bytes 4456448 | tf_op jit(solution)/shard_map/all_gather | solution.py:66
  584.6 54.2 %copy-start.17 = (pred[256]{0:T(512)(128)(4,1)S(1)}, pred[256]{0:T(512)(128)(4,1)}, u32[]{:S(2)}) copy-start(pred[256]{0:T(512)(128)(4,1)} %fusion.109) | copy-start | bytes 772
  634.8 3.3 copy-start.5
  636.4 1.7 copy-start.10
  636.5 63.5 %copy-start.16 = (s32[2,24]{1,0:T(2,128)S(1)}, s32[2,24]{1,0:T(2,128)}, u32[]{:S(2)}) copy-start(s32[2,24]{1,0:T(2,128)} %param.8) | copy-start | bytes 580
  639.6 99.8 %all-gather.9.cloned.1.call-start = ((), (), s32[]{:S(2)}) async-start(), calls=%async_computation.5 | async-start | bytes 5242880 | tf_op jit(solution)/shard_map/all_gather | solution.py:100
  739.4 1.9 slice-start
  773.5 125.4 %all-to-all-start = ((f32[256,32,256]{2,0,1:T(8,128)}), f32[256,32,256]{2,0,1:T(8,128)}, u32[]{:S(2)}, u32[]{:S(2)}) async-start(f32[256,32,256]{2,0,1:T(8,128)} %copy.64), calls=%async_computation | async-start | bytes 16777216 | tf_op jit(solution)/shard_map/all_to_all | solution.py:117
  780.6 449.5 %all-reduce.17.cloned.1.call-start = ((), (), s32[]{:S(2)}) async-start(), calls=%async_computation.8 | async-start | bytes 8388608 | tf_op jit(solution)/shard_map/psum | solution.py:16
  914.6 3.2 copy-start
  917.8 382.8 %all-reduce.15.cloned.1.call-start = ((), (), s32[]{:S(2)}) async-start(), calls=%async_computation.6 | async-start | bytes 2097152 | tf_op jit(solution)/shard_map/psum | solution.py:16
  1232.4 316.9 %all-gather.11.cloned.1.call-start = ((), (), s32[]{:S(2)}) async-start(), calls=%async_computation.7 | async-start | bytes 10485760 | tf_op jit(solution)/shard_map/all_gather | solution.py:64
  1328.7 14.6 copy-start.13
  1470.2 4.9 copy-start.15
  1472.6 3.6 copy-start.4
  1476.2 8.0 copy-start.1
  1479.7 4.5 copy-start.2
  1484.2 1.0 copy-start.3
  (6 other events, 5.1 us)
Sparse Core Ops, SparseCore 0:
  11.1 45.8 all-reduce.10
  60.8 84.1 all-reduce.20
  301.9 57.2 all-gather.4
  362.2 42.9 all-reduce.12
  408.9 84.1 all-reduce.18
  639.7 57.2 all-gather.6
  700.0 39.3 all-gather.8
  917.9 312.1 all-reduce.16
  1233.2 67.3 all-reduce.14
  1487.1 62.1 all-gather.10
where the time goes:
time: 1580 us; the launch traced here: 1560 us
  waiting for transfers between devices  958 us (61%)
  other arithmetic  405 us (26%)
  local copies, waits for them, and re-layouts  101 us (6%)
  matrix products  68.5 us (4%)
  between operations  23.2 us (1%)
    psum x6, waiting for transfers between devices, from_root(): return lax.psum(block, axis)  642 us
    another operation x44, other arithmetic, panel_step(): diag_factor = jnp.linalg.cholesky(diagonal)  260 us
    another operation x7, other arithmetic, panel_step(): lax.linalg.triangular_solve(diag_factor, panel_rows, left_side=False, low...  120 us
    all_to_all x1, waiting for transfers between devices, local(): lax.all_to_all(placed, ('child', 'row'), split_axis=1, concat_axis=0, til...  116 us
    all_gather x2, waiting for transfers between devices, panel_step(): all_rows = lax.all_gather(update_rows, 'row', axis=0, tiled=True)  115 us
    all_gather x1, waiting for transfers between devices, panel_step(): all_rows = lax.all_gather(update_rows, 'col', axis=0, tiled=True)  46.4 us
    all_gather x1, waiting for transfers between devices, local(): full_rows = lax.all_gather(local_tile, 'col', axis=1, tiled=True)  39.3 us
  transfers between devices with their start and end apart: 11, of which 11 were waited for; matrix products, arithmetic and copies ran while one was open for 1% of the time, Pallas kernels for 0%

commit v1 on v0

--- a/solution.py
+++ b/solution.py
@@ -97,7 +97,9 @@
     row_targets = lookup(block_maps, source_child, contrib_rows)
     row_valid = contrib_rows >= 0
     block_ids = jnp.arange(root_blocks, dtype=jnp.int32)
-    full_rows = lax.all_gather(local_tile, "col", axis=1, tiled=True)
+    full_rows = jnp.concatenate(
+        lax.all_to_all(jnp.stack([local_tile] * lax.axis_size("col")), "col", 0, 0), axis=1
+    )
     contrib = full_rows[:, PIV:].reshape(row_block, NCB, BLK)
     col_targets = lookup(
         block_maps, jnp.full((NCB,), child_pos, dtype=jnp.int32), jnp.arange(NCB, dtype=jnp.int32)

time: 1580 us -> 1590 us (level)
    all_to_all x0 -> x1, waiting for transfers between devices: none -> 48.6 us  [local(): lax.all_to_all(jnp.stack([local_tile] * lax.axis_size('col')), 'col', 0, 0)]
    all_gather x1 -> x0, waiting for transfers between devices: 39.3 us -> none  [local(): full_rows = lax.all_gather(local_tile, 'col', axis=1, tiled=True)]
where the time goes in v1:
time: 1590 us; the launch traced here: 1580 us
  waiting for transfers between devices  962 us (61%)
  other arithmetic  405 us (25%)
  local copies, waits for them, and re-layouts  109 us (7%)
  matrix products  67.5 us (4%)
  between operations  22.9 us (1%)
    psum x6, waiting for transfers between devices, from_root(): return lax.psum(block, axis)  644 us
    another operation x44, other arithmetic, panel_step(): diag_factor = jnp.linalg.cholesky(diagonal)  260 us
    another operation x7, other arithmetic, panel_step(): lax.linalg.triangular_solve(diag_factor, panel_rows, left_side=False, low...  120 us
    all_gather x2, waiting for transfers between devices, panel_step(): all_rows = lax.all_gather(update_rows, 'row', axis=0, tiled=True)  115 us
    all_to_all x1, waiting for transfers between devices, local(): lax.all_to_all(placed, ('child', 'row'), split_axis=1, concat_axis=0, til...  109 us
    all_to_all x1, waiting for transfers between devices, local(): lax.all_to_all(jnp.stack([local_tile] * lax.axis_size('col')), 'col', 0, 0)  48.6 us
    all_gather x1, waiting for transfers between devices, panel_step(): all_rows = lax.all_gather(update_rows, 'col', axis=0, tiled=True)  46.4 us
  transfers between devices with their start and end apart: 11, of which 11 were waited for; matrix products, arithmetic and copies ran while one was open for 1% of the time, Pallas kernels for 0%

profile of v1, /device:TPU:1, one launch (start us, length us, event | category | flops | bytes accessed | tf_op | source)
XLA Modules:
  0.0 1581.3 jit_solution(14065528968426397484)
XLA Ops:
  9.7 47.3 %all-reduce.11.cloned.1.call-done = f32[256,512]{0,1:T(8,128)} async-done(((f32[256,512]{0,1:T(8,128)}), f32[256,512]{0,1:T(8,128)}) %all-reduce.11.cloned.1.call-update) | async-done | bytes 524304 | tf_op jit(solution)/shard_map/psum | solution.py:16
  59.1 85.8 %all-reduce.21.cloned.1.call-done = (f32[256,512]{0,1:T(8,128)}, f32[256,512]{0,1:T(8,128)}) async-done(((f32[256,512]{0,1:T(8,128)}, f32[256,512]{0,1:T(8,128)}), (f32[256,512]{0,1:T(8,128)}, f32[256,512]{0,1:T(8,128)})) %all-reduce.21.cloned.1.call-update) | async-done | bytes 1048592 | tf_op jit(solution)/shard_map/psum | solution.py:16
  148.8 11.7 cholesky.374
  173.0 11.7 cholesky.393
  196.3 11.7 cholesky.414
  220.1 11.7 cholesky.431
  232.4 12.5 compare_reduce_fusion.10
  255.7 39.3 %custom-call.37 = f32[4,128,128]{1,2,0:T(8,128)S(1)} custom-call(f32[4,128,128]{2,1,0:T(8,128)S(1)} %get-tuple-element.27), custom_call_target="InvertDiagBlocksLowerTriangular" | custom-call | tf_op jit(solution)/shard_map/triangular_solve/custom-call.3 | solution.py:57
  301.9 57.4 %all-gather.4.cloned.1.call-done = bf16[4096,512]{0,1:T(8,128)(2,1)} async-done(((bf16[256,512]{0,1:T(8,128)(2,1)}), bf16[4096,512]{0,1:T(8,128)(2,1)}) %all-gather.4.cloned.1.call-update) | async-done | bytes 4194320 | tf_op jit(solution)/shard_map/all_gather | solution.py:66
  362.0 43.1 %all-reduce.13.cloned.1.call-done = f32[256,512]{0,1:T(8,128)} async-done(((f32[256,512]{0,1:T(8,128)}), f32[256,512]{0,1:T(8,128)}) %all-reduce.13.cloned.1.call-update) | async-done | bytes 524304 | tf_op jit(solution)/shard_map/psum | solution.py:16
  407.9 85.2 %all-reduce.19.cloned.1.call-done = (f32[256,512]{0,1:T(8,128)}, f32[256,512]{0,1:T(8,128)}) async-done(((f32[256,512]{0,1:T(8,128)}, f32[256,512]{0,1:T(8,128)}), (f32[256,512]{0,1:T(8,128)}, f32[256,512]{0,1:T(8,128)})) %all-reduce.19.cloned.1.call-update) | async-done | bytes 1048592 | tf_op jit(solution)/shard_map/psum | solution.py:16
  496.8 11.7 cholesky.446
  521.0 11.7 cholesky.465
  592.6 39.3 %custom-call.41 = f32[4,128,128]{1,2,0:T(8,128)S(1)} custom-call(f32[4,128,128]{2,1,0:T(8,128)S(1)} %get-tuple-element.28), custom_call_target="InvertDiagBlocksLowerTriangular" | custom-call | tf_op jit(solution)/shard_map/triangular_solve/custom-call.3 | solution.py:57
  639.4 57.4 %all-gather.6.cloned.1.call-done = bf16[4096,512]{0,1:T(8,128)(2,1)} async-done(((bf16[256,512]{0,1:T(8,128)(2,1)}), bf16[4096,512]{0,1:T(8,128)(2,1)}) %all-gather.6.cloned.1.call-update) | async-done | bytes 4194320 | tf_op jit(solution)/shard_map/all_gather | solution.py:66
  708.5 48.6 %all-to-all-done = f32[4,256,1024]{2,1,0:T(8,128)} async-done(((f32[4,256,1024]{2,1,0:T(8,128)}), f32[4,256,1024]{2,1,0:T(8,128)}, u32[]{:S(2)}, u32[]{:S(2)}) %all-to-all-start) | async-done | bytes 4194336 | tf_op jit(solution)/shard_map/all_to_all | solution.py:101
  805.1 108.7 %all-to-all-done.1 = f32[256,32,256]{2,0,1:T(8,128)} async-done(((f32[256,32,256]{2,0,1:T(8,128)}), f32[256,32,256]{2,0,1:T(8,128)}, u32[]{:S(2)}, u32[]{:S(2)}) %all-to-all-start.1) | async-done | bytes 8388640 | tf_op jit(solution)/shard_map/all_to_all | solution.py:119
  932.7 314.8 %all-reduce.17.cloned.1.call-done = (f32[2048,256]{0,1:T(8,128)}, f32[2048,256]{0,1:T(8,128)}) async-done(((f32[2048,256]{0,1:T(8,128)}, f32[2048,256]{0,1:T(8,128)}), (f32[2048,256]{0,1:T(8,128)}, f32[2048,256]{0,1:T(8,128)})) %all-reduce.17.cloned.1.call-update) | async-done | bytes 4194320 | tf_op jit(solution)/shard_map/psum | solution.py:16
  1250.3 67.6 %all-reduce.15.cloned.1.call-done = f32[512,512]{0,1:T(8,128)} async-done(((f32[512,512]{0,1:T(8,128)}), f32[512,512]{0,1:T(8,128)}) %all-reduce.15.cloned.1.call-update) | async-done | bytes 1048592 | tf_op jit(solution)/shard_map/psum | solution.py:16
  1377.9 13.2 cholesky.558
  1409.9 13.2 cholesky.575
  1435.3 12.0 while.5
  1447.3 40.1 %custom-call.26 = f32[4,128,128]{1,2,0:T(8,128)} custom-call(f32[4,128,128]{2,1,0:T(8,128)S(1)} %get-tuple-element.20), custom_call_target="InvertDiagBlocksLowerTriangular" | custom-call | tf_op jit(solution)/shard_map/triangular_solve | solution.py:57
  1520.2 46.4 %all-gather.8.cloned.1.call-done = bf16[8192,512]{0,1:T(8,128)(2,1)} async-done(((bf16[2048,512]{0,1:T(8,128)(2,1)}), bf16[8192,512]{0,1:T(8,128)(2,1)}) %all-gather.8.cloned.1.call-update) | async-done | bytes 8388624 | tf_op jit(solution)/shard_map/all_gather | solution.py:64
  (262 shorter events, 383.9 us)
Async XLA Ops:
  7.2 49.8 %all-reduce.11.cloned.1.call-start = ((), (), s32[]{:S(2)}) async-start(), calls=%async_computation.2 | async-start | bytes 1048576 | tf_op jit(solution)/shard_map/psum | solution.py:16
  9.6 135.3 %all-reduce.21.cloned.1.call-start = ((), (), s32[]{:S(2)}) async-start(), calls=%async_computation.10 | async-start | bytes 2097152 | tf_op jit(solution)/shard_map/psum | solution.py:16
  59.1 300.2 %all-gather.4.cloned.1.call-start = ((), (), s32[]{:S(2)}) async-start(), calls=%async_computation.3 | async-start | bytes 4456448 | tf_op jit(solution)/shard_map/all_gather | solution.py:66
  299.3 62.6 %copy-start.9 = (f32[256,128]{0,1:T(8,128)}, f32[256,128]{0,1:T(8,128)S(1)}, u32[]{:S(2)}) copy-start(f32[256,128]{0,1:T(8,128)S(1)} %fusion.81) | copy-start | bytes 393220
  301.8 103.3 %all-reduce.13.cloned.1.call-start = ((), (), s32[]{:S(2)}) async-start(), calls=%async_computation.4 | async-start | bytes 1048576 | tf_op jit(solution)/shard_map/psum | solution.py:16
  362.0 131.0 %all-reduce.19.cloned.1.call-start = ((), (), s32[]{:S(2)}) async-start(), calls=%async_computation.9 | async-start | bytes 2097152 | tf_op jit(solution)/shard_map/psum | solution.py:16
  407.3 289.6 %all-gather.6.cloned.1.call-start = ((), (), s32[]{:S(2)}) async-start(), calls=%async_computation.5 | async-start | bytes 4456448 | tf_op jit(solution)/shard_map/all_gather | solution.py:66
  495.8 1.0 copy-start.6
  584.5 54.2 %copy-start.17 = (pred[256]{0:T(512)(128)(4,1)S(1)}, pred[256]{0:T(512)(128)(4,1)}, u32[]{:S(2)}) copy-start(pred[256]{0:T(512)(128)(4,1)} %fusion.109) | copy-start | bytes 772
  634.7 3.3 copy-start.5
  636.3 1.7 copy-start.10
  701.6 6.7 copy-start.16
  701.6 55.6 %all-to-all-start = ((f32[4,256,1024]{2,1,0:T(8,128)}), f32[4,256,1024]{2,1,0:T(8,128)}, u32[]{:S(2)}, u32[]{:S(2)}) async-start(f32[4,256,1024]{2,1,0:T(8,128)} %stack.2), calls=%async_computation | async-start | bytes 8388608 | tf_op jit(solution)/shard_map/all_to_all | solution.py:101
  796.9 117.0 %all-to-all-start.1 = ((f32[256,32,256]{2,0,1:T(8,128)}), f32[256,32,256]{2,0,1:T(8,128)}, u32[]{:S(2)}, u32[]{:S(2)}) async-start(f32[256,32,256]{2,0,1:T(8,128)} %copy.134), calls=%async_computation.1 | async-start | bytes 16777216 | tf_op jit(solution)/shard_map/all_to_all | solution.py:119
  802.9 444.6 %all-reduce.17.cloned.1.call-start = ((), (), s32[]{:S(2)}) async-start(), calls=%async_computation.8 | async-start | bytes 8388608 | tf_op jit(solution)/shard_map/psum | solution.py:16
  929.5 3.2 copy-start
  932.7 385.2 %all-reduce.15.cloned.1.call-start = ((), (), s32[]{:S(2)}) async-start(), calls=%async_computation.6 | async-start | bytes 2097152 | tf_op jit(solution)/shard_map/psum | solution.py:16
  1249.8 316.8 %all-gather.8.cloned.1.call-start = ((), (), s32[]{:S(2)}) async-start(), calls=%async_computation.7 | async-start | bytes 10485760 | tf_op jit(solution)/shard_map/all_gather | solution.py:64
  1345.9 14.6 copy-start.13
  1487.4 4.9 copy-start.15
  1489.8 3.6 copy-start.4
  1493.4 8.0 copy-start.1
  1496.9 4.5 copy-start.2
  1501.4 1.0 copy-start.3
  (5 other events, 4.1 us)
Sparse Core Ops, SparseCore 0:
  11.1 45.8 all-reduce.10
  60.8 84.1 all-reduce.20
  301.9 57.2 all-gather.3
  362.2 42.9 all-reduce.12
  408.9 84.1 all-reduce.18
  639.5 57.2 all-gather.5
  932.8 314.6 all-reduce.16
  1250.6 67.2 all-reduce.14
  1504.4 62.1 all-gather.7
